TPU v7x, 128 devices: a whole 4x4x4 slice. The times are simulated.
128 devices in a mesh: tx: 4 (over z), ty: 32 (over x, y, core).
Axes of the slice: x: 4, y: 4, z: 4, core: 2. Of those that a mesh axis runs over, the one named last changes fastest.
Arguments:
- points: bfloat16 [128, 1024, 256], P(('tx', 'ty')), may hold values from -6 to 6
- counts: int32 [128], P(('tx', 'ty')), may hold values from 512 to 1024, as said below
- owner: int32 [128, 1024], P(('tx', 'ty')), may hold values from 0 to 127, as said below
- zorder: int32 [128, 2048], P(('tx', 'ty')), may hold values from 0 to 2047, as said below
- border: int32 [128, 4, 64], P(('tx', 'ty')), may hold values from 0 to 1023, as said below
- near: int32 [128, 16, 1024], P(('tx', 'ty')), may hold values from 0 to 1279, as said below
- w_near: bfloat16 [256, 256], replicated, may hold values from -0.375 to 0.375
- gain_one: float32 [256], replicated, may hold values from 0.1 to 1.9
- conv_w: bfloat16 [3, 8, 32, 32], replicated, may hold values from -0.625 to 0.625
- gain_two: float32 [256], replicated, may hold values from 0.1 to 1.9
- w_up: bfloat16 [256, 1024], replicated, may hold values from -0.375 to 0.375
- w_down: bfloat16 [1024, 256], replicated, may hold values from -0.1875 to 0.1875
- grad_out: bfloat16 [128, 1024, 256], P(('tx', 'ty')), may hold values from -6 to 6
Outputs:
- out_rows: bfloat16 [128, 1024, 256], P(('tx', 'ty'))
- grad_points: bfloat16 [128, 1024, 256], P(('tx', 'ty'))
- grad_w_near: float32 [256, 256], replicated
- grad_gain_one: float32 [256], replicated
- grad_conv: float32 [3, 8, 32, 32], replicated
- grad_gain_two: float32 [256], replicated
- grad_w_up: float32 [256, 1024], replicated
- grad_w_down: float32 [1024, 256], replicated
Inputs may be any that keep to these rules, and one draw needn't show every extreme that they name: `counts`: every tile has at least half of its slots live, and some tile has all of them live. Only live rows count. Among the live rows of one tile at most 16 name the same owner. One particular owner receives exactly 16 live rows from every tile; every other owner receives at most 16 live rows from each tile, so its receive buffer may be partly empty. `zorder`: each owner's entry is a permutation of its 2048 receive slots whose first entries name exactly the filled slots. `border`: each list names distinct live rows of its tile; lists toward a side outside the grid are never read. `near`: indices below 1024 name live rows of the tile; the others name halo rows of blocks whose neighbour tile exists.
All inputs are finite; a program needn't handle non-finite values.
Results may differ from a plain program's by a relative error of at most 0.015.
Values may be sent and summed in bfloat16 or wider, within the bound.
A program may use at most 64 MiB of HBM per device.

v0:
```python
import math
import jax
import jax.numpy as jnp
from jax import lax
from jax.sharding import PartitionSpec as P

PATCH = 1024
eps_norm = 1e-06
gelu_coef = 0.7978845608028654
cubic_coef = 0.044715


def shifted(value, axis, steps):
    count = lax.axis_size(axis)
    initial, last = (max(0, -steps), min(count, count - steps))
    return lax.ppermute(value, axis, [(source, source + steps) for source in range(initial, last)])


def gelu_tanh(value):
    inner = gelu_coef * (value + cubic_coef * value * value * value)
    return 0.5 * value * (1.0 + jnp.tanh(inner))


def gelu_slope(value):
    inner = gelu_coef * (value + cubic_coef * value * value * value)
    tangent = jnp.tanh(inner)
    return 0.5 * (1.0 + tangent) + 0.5 * value * (1.0 - tangent * tangent) * gelu_coef * (
        1.0 + 3.0 * cubic_coef * value * value
    )


def inverse_rms(value):
    return lax.rsqrt(jnp.mean(value * value, axis=-1, keepdims=True) + eps_norm)


def near_counts(near_tile, ext_count):
    rows = lax.broadcasted_iota(jnp.int32, (ext_count, near_tile.shape[1]), 0)
    total = jnp.zeros((ext_count, near_tile.shape[1]), jnp.float32)
    for index in range(near_tile.shape[0]):
        total = total + (near_tile[index][None, :] == rows).astype(jnp.float32)
    return total.astype(jnp.bfloat16)


def tile_forward(points_tile, halo_rows, counts_t, w_near, count_near):
    extended = jnp.concatenate([points_tile, halo_rows], axis=0)
    total = lax.dot_general(
        counts_t, extended, (((0,), (0,)), ((), ())), preferred_element_type=jnp.float32
    )
    average = (total * (1.0 / count_near)).astype(jnp.bfloat16)
    linear_part = jnp.dot(average, w_near, preferred_element_type=jnp.float32)
    lifted = (points_tile.astype(jnp.float32) + gelu_tanh(linear_part)).astype(jnp.bfloat16)
    return (average, linear_part, lifted)


def tile_backward(lifted_grad, average, linear_part, counts_t, w_near, count_near):
    tile_rows = lifted_grad.shape[0]
    act_grad = (lifted_grad.astype(jnp.float32) * gelu_slope(linear_part)).astype(jnp.bfloat16)
    near_grad = lax.dot_general(
        average, act_grad, (((0,), (0,)), ((), ())), preferred_element_type=jnp.float32
    )
    spread = lax.dot_general(
        act_grad, w_near, (((1,), (1,)), ((), ())), preferred_element_type=jnp.float32
    ) * (1.0 / count_near)
    spread_hi = spread.astype(jnp.bfloat16)
    spread_lo = (spread - spread_hi.astype(jnp.float32)).astype(jnp.bfloat16)
    ext_grad = jnp.dot(counts_t, spread_hi, preferred_element_type=jnp.float32) + jnp.dot(
        counts_t, spread_lo, preferred_element_type=jnp.float32
    )
    row_grad = lifted_grad.astype(jnp.float32) + ext_grad[:tile_rows]
    halo_grad = ext_grad[tile_rows:].astype(jnp.bfloat16)
    return (near_grad, row_grad, halo_grad)


def route_ranks(owner_tile, count, tiles):
    tile_rows = owner_tile.shape[0]
    index = jnp.arange(tile_rows, dtype=jnp.int32)
    live = index < count
    score = jnp.where(live, owner_tile * tile_rows + index, tiles * tile_rows + index)
    order = jnp.argsort(score, stable=True)
    members = (owner_tile[:, None] == jnp.arange(tiles, dtype=jnp.int32)[None, :]) & live[:, None]
    per_owner = jnp.sum(members.astype(jnp.int32), axis=0)
    starts = jnp.cumsum(per_owner) - per_owner
    sorted_owner = jnp.take(owner_tile, order)
    ranked = index - jnp.take(starts, sorted_owner)
    rank = jnp.zeros((tile_rows,), jnp.int32).at[order].set(ranked)
    return (rank, live)


def shift_down(rows):
    patches = rows.reshape(-1, PATCH, rows.shape[-1])
    moved = jnp.concatenate([jnp.zeros_like(patches[:, :1]), patches[:, :-1]], axis=1)
    return moved.reshape(rows.shape)


def shift_up(rows):
    patches = rows.reshape(-1, PATCH, rows.shape[-1])
    moved = jnp.concatenate([patches[:, 1:], jnp.zeros_like(patches[:, :1])], axis=1)
    return moved.reshape(rows.shape)


def block_taps(conv_w):
    groups, inner = (conv_w.shape[1], conv_w.shape[2])
    identity_blocks = jnp.eye(groups, dtype=conv_w.dtype)
    full = jnp.einsum("gh,ogab->ogahb", identity_blocks, conv_w)
    return full.reshape(conv_w.shape[0], groups * inner, groups * inner)


def grouped_weight(inputs, outputs, groups, inner):
    length = inputs.shape[0]
    left = inputs.reshape(length, groups, inner)
    right = outputs.reshape(length, groups, inner)
    return jnp.einsum("pga,pgb->gab", left, right, preferred_element_type=jnp.float32)


def tap_back(rows, tap):
    return lax.dot_general(rows, tap, (((1,), (1,)), ((), ())), preferred_element_type=jnp.float32)


def patch_pass(serial, out_grad, gain_one, conv_w, taps_full, gain_two, w_up, w_down):
    groups, inner = (conv_w.shape[1], conv_w.shape[2])
    serial_f = serial.astype(jnp.float32)
    scale_one = inverse_rms(serial_f)
    normed = (serial_f * scale_one * gain_one).astype(jnp.bfloat16)
    taps = (shift_down(normed), normed, shift_up(normed))
    mixed = (
        jnp.dot(taps[0], taps_full[0], preferred_element_type=jnp.float32)
        + jnp.dot(taps[1], taps_full[1], preferred_element_type=jnp.float32)
        + jnp.dot(taps[2], taps_full[2], preferred_element_type=jnp.float32)
    )
    state = serial_f + mixed
    scale_two = inverse_rms(state)
    second = (state * scale_two * gain_two).astype(jnp.bfloat16)
    hidden_pre = jnp.dot(second, w_up, preferred_element_type=jnp.float32)
    hidden = gelu_tanh(hidden_pre).astype(jnp.bfloat16)
    result = (state + jnp.dot(hidden, w_down, preferred_element_type=jnp.float32)).astype(
        jnp.bfloat16
    )
    down_grad = lax.dot_general(
        hidden, out_grad, (((0,), (0,)), ((), ())), preferred_element_type=jnp.float32
    )
    hidden_grad = lax.dot_general(
        out_grad, w_down, (((1,), (1,)), ((), ())), preferred_element_type=jnp.float32
    ).astype(jnp.bfloat16)
    pre_grad = (hidden_grad.astype(jnp.float32) * gelu_slope(hidden_pre)).astype(jnp.bfloat16)
    up_grad = lax.dot_general(
        second, pre_grad, (((0,), (0,)), ((), ())), preferred_element_type=jnp.float32
    )
    second_grad = lax.dot_general(
        pre_grad, w_up, (((1,), (1,)), ((), ())), preferred_element_type=jnp.float32
    ).astype(jnp.bfloat16)
    unit_two = state * scale_two
    weighted_two = second_grad.astype(jnp.float32) * gain_two
    gain_two_grad = jnp.sum(second_grad.astype(jnp.float32) * unit_two, axis=0)
    state_grad = out_grad.astype(jnp.float32) + scale_two * (
        weighted_two - unit_two * jnp.mean(weighted_two * unit_two, axis=-1, keepdims=True)
    )
    mixed_grad = state_grad.astype(jnp.bfloat16)
    conv_grad = jnp.stack(
        [
            grouped_weight(taps[0], mixed_grad, groups, inner),
            grouped_weight(taps[1], mixed_grad, groups, inner),
            grouped_weight(taps[2], mixed_grad, groups, inner),
        ],
        axis=0,
    )
    normed_grad = (
        shift_up(tap_back(mixed_grad, taps_full[0]))
        + tap_back(mixed_grad, taps_full[1])
        + shift_down(tap_back(mixed_grad, taps_full[2]))
    ).astype(jnp.bfloat16)
    unit_one = serial_f * scale_one
    weighted_one = normed_grad.astype(jnp.float32) * gain_one
    gain_one_grad = jnp.sum(normed_grad.astype(jnp.float32) * unit_one, axis=0)
    serial_grad = (
        state_grad
        + scale_one
        * (weighted_one - unit_one * jnp.mean(weighted_one * unit_one, axis=-1, keepdims=True))
    ).astype(jnp.bfloat16)
    return (result, serial_grad, (gain_one_grad, conv_grad, gain_two_grad, up_grad, down_grad))


def pass_columns(rows, shift_by):
    return shifted(rows, "tx", shift_by)


def pass_lines(rows, shift_by):
    return shifted(rows, "ty", shift_by)


def body(
    points,
    counts,
    owner,
    zorder,
    border,
    near,
    w_near,
    gain_one,
    conv_w,
    gain_two,
    w_up,
    w_down,
    grad_out,
):
    points_tile = points[0]
    tile_rows, width = points_tile.shape
    lists = border[0]
    border_rows = lists.shape[1]
    cols_count = lax.axis_size("tx")
    lines_count = lax.axis_size("ty")
    tiles = cols_count * lines_count
    recv_rows = zorder.shape[1]
    capacity = recv_rows // tiles
    near_tile = near[0]
    owner_tile = owner[0]
    sent = jnp.take(points_tile, lists.reshape(-1), axis=0).reshape(4, border_rows, width)
    halo = jnp.concatenate(
        [
            pass_columns(sent[0], -1),
            pass_columns(sent[1], 1),
            pass_lines(sent[2], -1),
            pass_lines(sent[3], 1),
        ],
        axis=0,
    )
    count_near = near_tile.shape[0]
    counts_t = near_counts(near_tile, tile_rows + 4 * border_rows)
    average, linear_part, lifted = tile_forward(points_tile, halo, counts_t, w_near, count_near)
    rank, live = route_ranks(owner_tile, counts[0], tiles)
    slots = jnp.where(live, owner_tile * capacity + rank, tiles * capacity)
    payload = jnp.concatenate([lifted, grad_out[0]], axis=1)
    outgoing = (
        jnp.zeros((tiles * capacity, 2 * width), jnp.bfloat16).at[slots].set(payload, mode="drop")
    )
    incoming = lax.all_to_all(outgoing, ("tx", "ty"), split_axis=0, concat_axis=0, tiled=True)
    serial_both = jnp.take(incoming, zorder[0], axis=0)
    taps_full = block_taps(conv_w)
    results, serial_grads, sums = patch_pass(
        serial_both[:, :width],
        serial_both[:, width:],
        gain_one,
        conv_w,
        taps_full,
        gain_two,
        w_up,
        w_down,
    )
    back = jnp.concatenate(
        [results.reshape(recv_rows, width), serial_grads.reshape(recv_rows, width)], axis=1
    )
    back_slots = jnp.zeros_like(back).at[zorder[0]].set(back)
    returned = lax.all_to_all(back_slots, ("tx", "ty"), split_axis=0, concat_axis=0, tiled=True)
    back_rows = jnp.take(returned, slots, axis=0, mode="fill", fill_value=0)
    out_rows = back_rows[:, :width]
    lifted_grad = back_rows[:, width:]
    patch_flat = jnp.concatenate(
        [sums[0], sums[2], sums[1].reshape(-1), sums[3].reshape(-1), sums[4].reshape(-1)]
    )
    patch_total = lax.psum(patch_flat, ("tx", "ty"))
    near_grad, row_grad, halo_grad = tile_backward(
        lifted_grad, average, linear_part, counts_t, w_near, count_near
    )
    came_back = (
        pass_columns(halo_grad[0:border_rows], 1),
        pass_columns(halo_grad[border_rows : 2 * border_rows], -1),
        pass_lines(halo_grad[2 * border_rows : 3 * border_rows], 1),
        pass_lines(halo_grad[3 * border_rows : 4 * border_rows], -1),
    )
    for direction in range(4):
        row_grad = row_grad.at[lists[direction]].add(came_back[direction].astype(jnp.float32))
    row_grad, near_grad, patch_total = lax.optimization_barrier((row_grad, near_grad, patch_total))
    near_sum = lax.psum(near_grad, ("tx", "ty"))
    sizes = [width, width, conv_w.size, w_up.size, w_down.size]
    shapes = [(width,), (width,), conv_w.shape, w_up.shape, w_down.shape]
    offsets = [sum(sizes[:index]) for index in range(len(sizes))]
    gain_one_sum, gain_two_sum, conv_sum, up_sum, down_sum = [
        patch_total[start : start + size].reshape(shape)
        for start, size, shape in zip(offsets, sizes, shapes)
    ]
    totals = (gain_one_sum, conv_sum, gain_two_sum, up_sum, down_sum)
    scale = 1.0 / math.sqrt(tiles * tile_rows)
    return (
        out_rows[None],
        row_grad.astype(jnp.bfloat16)[None],
        near_sum * scale,
        totals[0] * scale,
        totals[1] * scale,
        totals[2] * scale,
        totals[3] * scale,
        totals[4] * scale,
    )


def solution(mesh):
    placed = (
        P(("tx", "ty"), None, None),
        P(("tx", "ty")),
        P(("tx", "ty"), None),
        P(("tx", "ty"), None),
        P(("tx", "ty"), None, None),
        P(("tx", "ty"), None, None),
        P(),
        P(),
        P(),
        P(),
        P(),
        P(),
        P(("tx", "ty"), None, None),
    )
    return jax.shard_map(
        body,
        mesh=mesh,
        in_specs=placed,
        out_specs=(
            P(("tx", "ty"), None, None),
            P(("tx", "ty"), None, None),
            P(),
            P(),
            P(),
            P(),
            P(),
            P(),
        ),
        check_vma=False,
    )
```

profile of v0, /device:TPU:1, one launch (start us, length us, event | category | flops | bytes accessed | tf_op | source)
XLA Modules:
  0.0 533.1 jit_solution(16888555418986480388)
XLA Ops:
  10.1 4.4 sort.17
  14.5 4.5 gather_fusion
  21.7 5.0 collective-permute-start.1
  26.7 2.9 collective-permute-start.2
  29.6 3.2 collective-permute-start.3
  33.7 6.6 %gather_fusion.1 = s32[1024]{0:T(1024)S(1)} fusion(s32[128]{0:T(128)S(1)} %sub.21, s32[1024]{0:T(1024)S(1)} %get-tuple-element.94), kind=kCustom, calls=%fused_computation.1 | custom fusion | bytes 12288 | tf_op jit(solution)/shard_map/jit(_take)/gather | solution.py:84
  40.3 4.3 scatter_custom_fusion
  44.6 10.6 %add_convert_fusion = bf16[1280,1024]{1,0:T(8,128)(2,1)S(1)} fusion(s32[1024]{0:T(1024)S(1)} %bitcast.175, s32[1024]{0:T(1024)S(1)} %bitcast.176, s32[1024]{0:T(1024)S(1)} %bitcast.162, s32[1024]{0:T(1024)S(1)} %bitcast.163, s32[1024]{0:T(1024)S(1)} %bitcast.164, s32[1024]{0:T(1024)S(1)} %bitcast.165, s32[1024]{0:T(1024)S(1)} %bitcast.166, ...), kind=kLoop, calls=%fused_computation.22 | loop fusion | flops 62914560 | bytes 2686976 | tf_op jit(solution)/shard_map/convert_element_type | solution.py:41
  57.0 1.5 add_convert_fusion.1
  58.5 6.8 %scatter_custom_fusion.1 = bf16[2048,512]{1,0:T(8,128)(2,1)} fusion(s32[1024]{0:T(1024)S(1)} %get-tuple-element.45, bf16[1024,256]{1,0:T(8,128)(2,1)S(1)} %bitcast.156, bf16[]{:T(256)} %constant.144, bf16[1024,256]{1,0:T(8,128)(2,1)S(1)} %get-tuple-element.85, bf16[]{:T(256)} %constant.59.clone.1), kind=kCustom, calls=%fused_computation.99 | custom fusion | flops 2097152 | bytes 3145732 | tf_op jit(solution)/shard_map/scatter | solution.py:233
  65.3 11.2 %all-to-all-start = ((bf16[128,16,512]{2,1,0:T(8,128)(2,1)}), bf16[128,16,512]{2,1,0:T(8,128)(2,1)S(1)}, u32[]{:S(2)}, u32[]{:S(2)}) async-start(bf16[128,16,512]{2,1,0:T(8,128)(2,1)} %bitcast.148), calls=%async_computation | async-start | bytes 4194304 | tf_op jit(solution)/shard_map/all_to_all | solution.py:235
  77.9 2.1 squeeze.54
  80.0 1.4 reshape.499
  82.1 1.4 squeeze.55
  84.2 22.8 %all-to-all-done = bf16[128,16,512]{2,1,0:T(8,128)(2,1)S(1)} async-done(((bf16[128,16,512]{2,1,0:T(8,128)(2,1)}), bf16[128,16,512]{2,1,0:T(8,128)(2,1)S(1)}, u32[]{:S(2)}, u32[]{:S(2)}) %all-to-all-start) | async-done | bytes 2097184 | tf_op jit(solution)/shard_map/all_to_all | solution.py:235
  107.0 9.2 %gather_fusion.3 = bf16[2048,512]{1,0:T(8,128)(2,1)} fusion(bf16[2048,512]{1,0:T(8,128)(2,1)S(1)} %bitcast.137, s32[2048]{0:T(1024)S(1)} %broadcast_clamp_fusion), kind=kCustom, calls=%fused_computation.3 | custom fusion | bytes 4202496 | tf_op jit(solution)/shard_map/jit(_take)/gather | solution.py:236
  116.2 4.0 copy.84
  120.2 1.8 broadcast_select_fusion
  122.3 1.4 fusion.24
  123.6 2.6 reshape.388
  126.3 4.1 fusion.70
  130.3 1.6 concatenate.26
  136.0 1.4 fusion.67
  137.5 6.5 %fusion.6 = bf16[2048,1024]{1,0:T(8,128)(2,1)S(1)} fusion(f32[2048,1024]{1,0:T(8,128)S(1)} %fusion.67, bf16[1024,256]{1,0:T(8,128)(2,1)S(1)} %copy-done.37, bf16[2048,512]{0,1:T(8,128)(2,1)S(1)} %broadcast_select_fusion), kind=kOutput, calls=%fused_computation.20 | convolution fusion | flops 1117782016 | bytes 14155776 | tf_op jit(solution)/shard_map/dot_general | solution.py:141
  144.0 2.3 convolution_bitcast_fusion.1
  146.2 2.6 fusion.23
  148.9 2.7 reshape_reshape.7
  151.6 2.6 reshape_reshape.6
  154.2 7.7 %fusion.13 = bf16[2048,256]{0,1:T(8,128)(2,1)} fusion(f32[2048,256]{0,1:T(8,128)} %copy-done.6, bf16[1024,256]{1,0:T(8,128)(2,1)S(1)} %copy-done.38, f32[2048,1024]{1,0:T(8,128)} %copy-done.12), kind=kOutput, calls=%fused_computation.56 | convolution fusion | flops 1093664768 | bytes 12058624 | tf_op jit(solution)/shard_map/dot_general | solution.py:135
  163.9 1.7 fusion.68
  165.7 2.3 copy.95
  167.9 1.7 fusion.37
  169.6 1.5 concatenate.28
  171.1 2.9 copy.93
  174.0 1.7 fusion.35
  175.7 1.5 concatenate.29
  177.2 2.9 copy.94
  180.1 3.6 fusion.26
  183.8 1.3 fusion.19
  185.4 2.7 copy.89
  188.1 11.5 %scatter_custom_fusion.2 = bf16[2048,512]{1,0:T(8,128)(2,1)} fusion(s32[2048]{0:T(1024)S(1)} %bitcast.160, bf16[2048,512]{1,0:T(8,128)(2,1)} %copy.89, bf16[]{:T(256)} %constant.59.clone.1), kind=kCustom, calls=%fused_computation.107 | custom fusion | bytes 2097664 | tf_op jit(solution)/shard_map/scatter | solution.py:251
  199.5 4.4 all-to-all-start.1
  204.0 2.1 convolution_bitcast_fusion.2
  207.1 5.6 %convolution_bitcast_fusion = f32[128,2,8,128]{3,2,1,0:T(8,128)S(1)} fusion(bf16[2048,512]{0,1:T(8,128)(2,1)} %copy-done.5, f32[2048,1024]{1,0:T(8,128)} %copy-done.12), kind=kOutput, calls=%fused_computation.79 | convolution fusion | flops 1092616192 | bytes 10485760 | tf_op jit(solution)/shard_map/dot_general | solution.py:138
  213.3 1.3 constant_dynamic-update-slice_fusion.5
  215.9 1.5 constant_dynamic-update-slice_fusion.8
  217.4 2.3 constant_dynamic-update-slice_fusion.7
  219.8 2.4 constant_dynamic-update-slice_fusion.6
  222.3 12.3 %all-to-all-done.1 = bf16[128,16,512]{2,1,0:T(8,128)(2,1)S(1)} async-done(((bf16[128,16,512]{2,1,0:T(8,128)(2,1)}), bf16[128,16,512]{2,1,0:T(8,128)(2,1)S(1)}, u32[]{:S(2)}, u32[]{:S(2)}) %all-to-all-start.1) | async-done | bytes 2097184 | tf_op jit(solution)/shard_map/all_to_all | solution.py:252
  234.6 5.1 gather_fusion.4
  239.6 1.5 broadcast_select_fusion.1
  244.7 1.9 collective-permute-start.4
  248.0 2.0 collective-permute-start.6
  250.0 2.8 collective-permute-start.7
  255.8 3.2 scatter_custom_fusion.3
  259.0 3.2 scatter_custom_fusion.4
  262.1 3.2 scatter_custom_fusion.5
  265.3 3.2 scatter_custom_fusion.6
  268.5 106.7 %all-reduce.7.cloned.1.call-done = f32[549376]{0:T(1024)} async-done(((f32[549376]{0:T(1024)}), f32[549376]{0:T(1024)}) %all-reduce.7.cloned.1.call-update) | async-done | bytes 2197520 | tf_op jit(solution)/shard_map/psum | solution.py:259
  375.2 2.7 slice_multiply_fusion
  378.9 2.4 mul.316
  384.4 1.3 slice_multiply_fusion.3
  385.7 138.7 %all-reduce.9.cloned.1.call-done = f32[256,256]{1,0:T(8,128)} async-done(((f32[256,256]{1,0:T(8,128)}), f32[256,256]{1,0:T(8,128)}) %all-reduce.9.cloned.1.call-update) | async-done | bytes 262160 | tf_op jit(solution)/shard_map/psum | solution.py:272
  524.4 1.7 broadcast_multiply_fusion
  (160 shorter events, 31.1 us)
Async XLA Ops:
  7.2 128.8 %copy-start = (bf16[256,1024]{1,0:T(8,128)(2,1)S(1)}, bf16[256,1024]{1,0:T(8,128)(2,1)}, u32[]{:S(2)}) copy-start(bf16[256,1024]{1,0:T(8,128)(2,1)} %param.23) | copy-start | bytes 1572868
  7.2 7.3 %copy-start.2 = (s32[1,1024]{1,0:T(1,128)S(1)}, s32[1,1024]{1,0:T(1,128)}, u32[]{:S(2)}) copy-start(s32[1,1024]{1,0:T(1,128)} %param.15) | copy-start | bytes 12292
  14.5 4.6 copy-start.15
  19.0 13.8 %copy-start.31 = (s32[1,16,1024]{2,1,0:T(8,128)S(1)}, s32[1,16,1024]{2,1,0:T(8,128)}, u32[]{:S(2)}) copy-start(s32[1,16,1024]{2,1,0:T(8,128)} %param.18) | copy-start | bytes 196612
  20.4 35.5 %collective-permute-start = (bf16[64,256]{1,0:T(8,128)(2,1)S(1)}, bf16[64,256]{1,0:T(8,128)(2,1)S(1)}, u32[]{:S(2)}, u32[]{:S(2)}) collective-permute-start(bf16[64,256]{1,0:T(8,128)(2,1)S(1)} %get-tuple-element.62), channel_id=1, source_target_pairs={{32,0},{64,32},{96,64},{33,1},{65,33},{97,65},{34,2},{66,34},{98,6... | collective-permute-start | bytes 98312 | tf_op jit(solution)/shard_map/ppermute | solution.py:16
  21.7 34.2 %collective-permute-start.1 = (bf16[64,256]{1,0:T(8,128)(2,1)S(1)}, bf16[64,256]{1,0:T(8,128)(2,1)S(1)}, u32[]{:S(2)}, u32[]{:S(2)}) collective-permute-start(bf16[64,256]{1,0:T(8,128)(2,1)S(1)} %get-tuple-element.61), channel_id=1, source_target_pairs={{0,32},{32,64},{64,96},{1,33},{33,65},{65,97},{2,34},{34,66},{66,9... | collective-permute-start | bytes 98312 | tf_op jit(solution)/shard_map/ppermute | solution.py:16
  26.7 29.2 %collective-permute-start.2 = (bf16[64,256]{1,0:T(8,128)(2,1)S(1)}, bf16[64,256]{1,0:T(8,128)(2,1)S(1)}, u32[]{:S(2)}, u32[]{:S(2)}) collective-permute-start(bf16[64,256]{1,0:T(8,128)(2,1)S(1)} %get-tuple-element.60), channel_id=1, source_target_pairs={{1,0},{2,1},{3,2},{4,3},{5,4},{6,5},{7,6},{8,7},{9,8},{10,9},{11,1... | collective-permute-start | bytes 98312 | tf_op jit(solution)/shard_map/ppermute | solution.py:16
  29.6 26.3 %collective-permute-start.3 = (bf16[64,256]{1,0:T(8,128)(2,1)S(1)}, bf16[64,256]{1,0:T(8,128)(2,1)S(1)}, u32[]{:S(2)}, u32[]{:S(2)}) collective-permute-start(bf16[64,256]{1,0:T(8,128)(2,1)S(1)} %get-tuple-element.59), channel_id=1, source_target_pairs={{0,1},{1,2},{2,3},{3,4},{4,5},{5,6},{6,7},{7,8},{8,9},{9,10},{10,1... | collective-permute-start | bytes 98312 | tf_op jit(solution)/shard_map/ppermute | solution.py:16
  55.2 1.6 copy-start.3
  55.9 1.1 copy-start.29
  57.0 1.5 copy-start.25
  57.0 1.5 copy-start.27
  65.3 11.2 %copy-start.28 = (bf16[3,8,32,32]{3,2,1,0:T(8,128)(2,1)S(1)}, bf16[3,8,32,32]{3,2,1,0:T(8,128)(2,1)}, u32[]{:S(2)}) copy-start(bf16[3,8,32,32]{3,2,1,0:T(8,128)(2,1)} %param.21) | copy-start | bytes 147460
  65.3 41.7 %all-to-all-start = ((bf16[128,16,512]{2,1,0:T(8,128)(2,1)}), bf16[128,16,512]{2,1,0:T(8,128)(2,1)S(1)}, u32[]{:S(2)}, u32[]{:S(2)}) async-start(bf16[128,16,512]{2,1,0:T(8,128)(2,1)} %bitcast.148), calls=%async_computation | async-start | bytes 4194304 | tf_op jit(solution)/shard_map/all_to_all | solution.py:235
  77.8 5.7 %copy-start.33 = (s32[1,4,64]{2,1,0:T(4,128)S(1)}, s32[1,4,64]{2,1,0:T(4,128)}, u32[]{:S(2)}) copy-start(s32[1,4,64]{2,1,0:T(4,128)} %param.17) | copy-start | bytes 3076
  77.8 6.3 %copy-start.32 = (s32[1,2048]{1,0:T(1,128)S(1)}, s32[1,2048]{1,0:T(1,128)}, u32[]{:S(2)}) copy-start(s32[1,2048]{1,0:T(1,128)} %param.16) | copy-start | bytes 24580
  120.2 2.1 copy-start.35
  122.0 61.8 %copy-start.5 = (bf16[2048,512]{0,1:T(8,128)(2,1)}, bf16[2048,512]{0,1:T(8,128)(2,1)S(1)}, u32[]{:S(2)}) copy-start(bf16[2048,512]{0,1:T(8,128)(2,1)S(1)} %broadcast_select_fusion) | copy-start | bytes 6291460
  132.0 1.2 copy-start.13
  132.3 1.2 copy-start.24
  133.2 1.0 copy-start.14
  133.4 1.3 copy-start.10
  135.3 0.7 copy-start.34
  136.0 10.3 %copy-start.6 = (f32[2048,256]{0,1:T(8,128)}, f32[2048,256]{0,1:T(8,128)S(1)}, u32[]{:S(2)}) copy-start(f32[2048,256]{0,1:T(8,128)S(1)} %get-tuple-element.88) | copy-start | bytes 6291460
  136.0 1.4 copy-start.37
  137.5 6.5 %copy-start.12 = (f32[2048,1024]{1,0:T(8,128)}, f32[2048,1024]{1,0:T(8,128)S(1)}, u32[]{:S(2)}) copy-start(f32[2048,1024]{1,0:T(8,128)S(1)} %fusion.67) | copy-start | bytes 25165828
  148.9 5.3 copy-start.38
  154.2 7.7 %copy-start.22 = (f32[32,8,8,128]{3,2,1,0:T(8,128)S(1)}, f32[32,8,8,128]{3,2,1,0:T(8,128)}, u32[]{:S(2)}) copy-start(f32[32,8,8,128]{3,2,1,0:T(8,128)} %convolution_bitcast_fusion.1) | copy-start | bytes 3145732
  154.2 8.9 %copy-start.19 = (bf16[2048,256]{0,1:T(8,128)(2,1)S(1)}, bf16[2048,256]{0,1:T(8,128)(2,1)}, u32[]{:S(2)}) copy-start(bf16[2048,256]{0,1:T(8,128)(2,1)} %get-tuple-element.89) | copy-start | bytes 3145732
  161.9 2.0 copy-start.7
  180.1 3.6 copy-start.8
  180.1 3.6 copy-start.20
  183.8 1.4 copy-start.23
  199.5 35.0 %all-to-all-start.1 = ((bf16[128,16,512]{2,1,0:T(8,128)(2,1)}), bf16[128,16,512]{2,1,0:T(8,128)(2,1)S(1)}, u32[]{:S(2)}, u32[]{:S(2)}) async-start(bf16[128,16,512]{2,1,0:T(8,128)(2,1)} %bitcast.147), calls=%async_computation.1 | async-start | bytes 4194304 | tf_op jit(solution)/shard_map/all_to_all | solution.py:252
  203.9 171.3 %all-reduce.7.cloned.1.call-start = ((), (), s32[]{:S(2)}) async-start(), calls=%async_computation.2 | async-start | bytes 4399104 | tf_op jit(solution)/shard_map/psum | solution.py:259
  203.9 2.1 copy-start.9
  204.0 2.2 copy-start.17
  204.0 2.6 copy-start.11
  212.8 4.7 copy-start.16
  222.2 302.2 %all-reduce.9.cloned.1.call-start = ((), (), s32[]{:S(2)}) async-start(), calls=%async_computation.3 | async-start | bytes 524288 | tf_op jit(solution)/shard_map/psum | solution.py:272
  234.6 5.1 copy-start.36
  239.6 1.6 copy-start.21
  239.6 2.3 copy-start.30
  241.2 1.8 copy-start.4
  243.8 9.0 %copy-start.26 = (bf16[1024,256]{1,0:T(8,128)(2,1)S(1)}, bf16[1024,256]{1,0:T(8,128)(2,1)}, u32[]{:S(2)}) copy-start(bf16[1024,256]{1,0:T(8,128)(2,1)} %copy-done.25) | copy-start | bytes 1572868
  244.7 11.1 %collective-permute-start.4 = (bf16[64,256]{1,0:T(8,128)(2,1)S(1)}, bf16[64,256]{1,0:T(8,128)(2,1)S(1)}, u32[]{:S(2)}, u32[]{:S(2)}) collective-permute-start(bf16[64,256]{1,0:T(8,128)(2,1)S(1)} %get-tuple-element.58), channel_id=1, source_target_pairs={{0,32},{32,64},{64,96},{1,33},{33,65},{65,97},{2,34},{34,66},{66,9... | collective-permute-start | bytes 98312 | tf_op jit(solution)/shard_map/ppermute | solution.py:16
  246.7 12.3 %collective-permute-start.5 = (bf16[64,256]{1,0:T(8,128)(2,1)S(1)}, bf16[64,256]{1,0:T(8,128)(2,1)S(1)}, u32[]{:S(2)}, u32[]{:S(2)}) collective-permute-start(bf16[64,256]{1,0:T(8,128)(2,1)S(1)} %get-tuple-element.57), channel_id=1, source_target_pairs={{32,0},{64,32},{96,64},{33,1},{65,33},{97,65},{34,2},{66,34},{98,6... | collective-permute-start | bytes 98312 | tf_op jit(solution)/shard_map/ppermute | solution.py:16
  248.0 14.2 %collective-permute-start.6 = (bf16[64,256]{1,0:T(8,128)(2,1)S(1)}, bf16[64,256]{1,0:T(8,128)(2,1)S(1)}, u32[]{:S(2)}, u32[]{:S(2)}) collective-permute-start(bf16[64,256]{1,0:T(8,128)(2,1)S(1)} %get-tuple-element.56), channel_id=1, source_target_pairs={{0,1},{1,2},{2,3},{3,4},{4,5},{5,6},{6,7},{7,8},{8,9},{9,10},{10,1... | collective-permute-start | bytes 98312 | tf_op jit(solution)/shard_map/ppermute | solution.py:16
  250.0 15.3 %collective-permute-start.7 = (bf16[64,256]{1,0:T(8,128)(2,1)S(1)}, bf16[64,256]{1,0:T(8,128)(2,1)S(1)}, u32[]{:S(2)}, u32[]{:S(2)}) collective-permute-start(bf16[64,256]{1,0:T(8,128)(2,1)S(1)} %get-tuple-element.55), channel_id=1, source_target_pairs={{1,0},{2,1},{3,2},{4,3},{5,4},{6,5},{7,6},{8,7},{9,8},{10,9},{11,1... | collective-permute-start | bytes 98312 | tf_op jit(solution)/shard_map/ppermute | solution.py:16
  378.9 3.7 copy-start.18
  381.3 144.7 %copy-start.1 = (bf16[256,1024]{1,0:T(8,128)(2,1)S(1)}, bf16[256,1024]{1,0:T(8,128)(2,1)}, u32[]{:S(2)}) copy-start(bf16[256,1024]{1,0:T(8,128)(2,1)} %param.23) | copy-start | bytes 1572868
Sparse Core Ops, SparseCore 0:
  222.3 152.8 all-reduce.6
  384.5 139.8 all-reduce.8
where the time goes:
time: 543 us; the launch traced here: 533 us
  waiting for transfers between devices  281 us (52%)
  local copies, waits for them, and re-layouts  102 us (19%)
  other arithmetic  55.1 us (10%)
  matrix products  43.2 us (8%)
  starting transfers between devices  36 us (7%)
  between operations  15.8 us (3%)
    psum x1, waiting for transfers between devices, body(): near_sum = lax.psum(near_grad, ('tx', 'ty'))  139 us
    psum x1, waiting for transfers between devices, body(): patch_total = lax.psum(patch_flat, ('tx', 'ty'))  107 us
    all_to_all x1, waiting for transfers between devices, body(): lax.all_to_all(outgoing, ('tx', 'ty'), split_axis=0, concat_axis=0, tiled...  22.8 us
    ppermute x8, starting transfers between devices, shifted(): lax.ppermute(value, axis, [(source, source + steps) for source in range(i...  20.4 us
    gather x2, local copies, waits for them, and re-layouts, body(): serial_both = jnp.take(incoming, zorder[0], axis=0)  13.1 us
    scatter-add x4, other arithmetic, body(): row_grad.at[lists[direction]].add(came_back[direction].astype(jnp.float32))  12.7 us
    all_to_all x1, waiting for transfers between devices, body(): lax.all_to_all(back_slots, ('tx', 'ty'), split_axis=0, concat_axis=0, til...  12.3 us
    scatter x1, local copies, waits for them, and re-layouts, body(): back_slots = jnp.zeros_like(back).at[zorder[0]].set(back)  11.5 us
  transfers between devices with their start and end apart: 12, of which 4 were waited for; matrix products, arithmetic and copies ran while one was open for 14% of the time, Pallas kernels for 0%

commit v1 on v0

--- a/solution.py
+++ b/solution.py
@@ -256,7 +256,7 @@
     patch_flat = jnp.concatenate(
         [sums[0], sums[2], sums[1].reshape(-1), sums[3].reshape(-1), sums[4].reshape(-1)]
     )
-    patch_total = lax.psum(patch_flat, ("tx", "ty"))
+    patch_total = lax.psum(lax.psum(patch_flat, "tx"), "ty")
     near_grad, row_grad, halo_grad = tile_backward(
         lifted_grad, average, linear_part, counts_t, w_near, count_near
     )

time: 543 us -> 565 us (1.041)
  waiting for transfers between devices: 281 us -> 295 us
    psum x1 -> x2, waiting for transfers between devices: 107 us -> 115 us  [body(): patch_total = lax.psum(lax.psum(patch_flat, 'tx'), 'ty')]
    unnamed x90 -> x92, local copies, waits for them, and re-layouts: 11.4 us -> 14 us
  transfers between devices with their start and end apart: 12 -> 13, of which waited for: 4 -> 5; matrix products, arithmetic and copies ran while one was open for 14% -> 13% of each run, Pallas kernels for 0% -> 0%
where the time goes in v1:
time: 565 us; the launch traced here: 555 us
  waiting for transfers between devices  295 us (52%)
  local copies, waits for them, and re-layouts  105 us (19%)
  other arithmetic  54.6 us (10%)
  matrix products  47.3 us (8%)
  starting transfers between devices  37.3 us (7%)
  between operations  15.5 us (3%)
    psum x1, waiting for transfers between devices, body(): near_sum = lax.psum(near_grad, ('tx', 'ty'))  140 us
    psum x2, waiting for transfers between devices, body(): patch_total = lax.psum(lax.psum(patch_flat, 'tx'), 'ty')  115 us
    all_to_all x1, waiting for transfers between devices, body(): lax.all_to_all(outgoing, ('tx', 'ty'), split_axis=0, concat_axis=0, tiled...  23.4 us
    ppermute x8, starting transfers between devices, shifted(): lax.ppermute(value, axis, [(source, source + steps) for source in range(i...  21.7 us
    all_to_all x1, waiting for transfers between devices, body(): lax.all_to_all(back_slots, ('tx', 'ty'), split_axis=0, concat_axis=0, til...  16.4 us
    unnamed x92, local copies, waits for them, and re-layouts  14 us
    gather x2, local copies, waits for them, and re-layouts, body(): serial_both = jnp.take(incoming, zorder[0], axis=0)  13.1 us
    scatter-add x4, other arithmetic, body(): row_grad.at[lists[direction]].add(came_back[direction].astype(jnp.float32))  12.3 us
  transfers between devices with their start and end apart: 13, of which 5 were waited for; matrix products, arithmetic and copies ran while one was open for 13% of the time, Pallas kernels for 0%

profile of v1, /device:TPU:1, one launch (start us, length us, event | category | flops | bytes accessed | tf_op | source)
XLA Modules:
  0.0 554.7 jit_solution(15408488579895970437)
XLA Ops:
  10.1 4.4 sort.17
  14.5 4.5 gather_fusion
  21.7 5.0 collective-permute-start.1
  26.7 2.9 collective-permute-start.2
  29.6 3.2 collective-permute-start.3
  33.7 6.6 %gather_fusion.1 = s32[1024]{0:T(1024)S(1)} fusion(s32[128]{0:T(128)S(1)} %sub.21, s32[1024]{0:T(1024)S(1)} %get-tuple-element.94), kind=kCustom, calls=%fused_computation.1 | custom fusion | bytes 12288 | tf_op jit(solution)/shard_map/jit(_take)/gather | solution.py:84
  40.3 4.3 scatter_custom_fusion
  44.6 10.6 %add_convert_fusion = bf16[1280,1024]{1,0:T(8,128)(2,1)S(1)} fusion(s32[1024]{0:T(1024)S(1)} %bitcast.175, s32[1024]{0:T(1024)S(1)} %bitcast.176, s32[1024]{0:T(1024)S(1)} %bitcast.162, s32[1024]{0:T(1024)S(1)} %bitcast.163, s32[1024]{0:T(1024)S(1)} %bitcast.164, s32[1024]{0:T(1024)S(1)} %bitcast.165, s32[1024]{0:T(1024)S(1)} %bitcast.166, ...), kind=kLoop, calls=%fused_computation.22 | loop fusion | flops 62914560 | bytes 2686976 | tf_op jit(solution)/shard_map/convert_element_type | solution.py:41
  56.8 1.4 add_convert_fusion.1
  58.2 6.8 %scatter_custom_fusion.1 = bf16[2048,512]{1,0:T(8,128)(2,1)} fusion(s32[1024]{0:T(1024)S(1)} %get-tuple-element.45, bf16[1024,256]{1,0:T(8,128)(2,1)S(1)} %bitcast.156, bf16[]{:T(256)} %constant.144, bf16[1024,256]{1,0:T(8,128)(2,1)S(1)} %get-tuple-element.85, bf16[]{:T(256)} %constant.59.clone.1), kind=kCustom, calls=%fused_computation.99 | custom fusion | flops 2097152 | bytes 3145732 | tf_op jit(solution)/shard_map/scatter | solution.py:233
  65.1 11.2 %all-to-all-start = ((bf16[128,16,512]{2,1,0:T(8,128)(2,1)}), bf16[128,16,512]{2,1,0:T(8,128)(2,1)S(1)}, u32[]{:S(2)}, u32[]{:S(2)}) async-start(bf16[128,16,512]{2,1,0:T(8,128)(2,1)} %bitcast.148), calls=%async_computation | async-start | bytes 4194304 | tf_op jit(solution)/shard_map/all_to_all | solution.py:235
  77.6 2.1 squeeze.54
  81.9 1.4 squeeze.55
  83.4 23.4 %all-to-all-done = bf16[128,16,512]{2,1,0:T(8,128)(2,1)S(1)} async-done(((bf16[128,16,512]{2,1,0:T(8,128)(2,1)}), bf16[128,16,512]{2,1,0:T(8,128)(2,1)S(1)}, u32[]{:S(2)}, u32[]{:S(2)}) %all-to-all-start) | async-done | bytes 2097184 | tf_op jit(solution)/shard_map/all_to_all | solution.py:235
  106.8 9.1 %gather_fusion.3 = bf16[2048,512]{1,0:T(8,128)(2,1)} fusion(bf16[2048,512]{1,0:T(8,128)(2,1)S(1)} %bitcast.137, s32[2048]{0:T(1024)S(1)} %broadcast_clamp_fusion), kind=kCustom, calls=%fused_computation.3 | custom fusion | bytes 4202496 | tf_op jit(solution)/shard_map/jit(_take)/gather | solution.py:236
  116.0 4.0 copy.84
  119.9 1.8 broadcast_select_fusion
  123.2 2.6 reshape.388
  125.9 4.1 fusion.70
  129.9 1.6 concatenate.26
  137.1 6.3 %fusion.6 = bf16[2048,1024]{1,0:T(8,128)(2,1)S(1)} fusion(f32[2048,1024]{1,0:T(8,128)S(1)} %fusion.67, bf16[1024,256]{1,0:T(8,128)(2,1)S(1)} %copy-done.38, bf16[2048,512]{0,1:T(8,128)(2,1)S(1)} %broadcast_select_fusion), kind=kOutput, calls=%fused_computation.20 | convolution fusion | flops 1117782016 | bytes 14155776 | tf_op jit(solution)/shard_map/dot_general | solution.py:141
  143.4 2.3 convolution_bitcast_fusion.1
  145.7 2.7 fusion.23
  148.3 2.6 reshape_reshape.7
  150.9 2.6 reshape_reshape.6
  153.6 6.4 %convolution_bitcast_fusion = f32[128,2,8,128]{3,2,1,0:T(8,128)} fusion(bf16[2048,512]{0,1:T(8,128)(2,1)S(1)} %broadcast_select_fusion, f32[2048,1024]{1,0:T(8,128)} %copy-done.11), kind=kOutput, calls=%fused_computation.79 | convolution fusion | flops 1092616192 | bytes 10485760 | tf_op jit(solution)/shard_map/dot_general | solution.py:138
  160.0 6.9 %fusion.13 = bf16[2048,256]{0,1:T(8,128)(2,1)} fusion(f32[2048,256]{0,1:T(8,128)S(1)} %copy-done.6, bf16[1024,256]{1,0:T(8,128)(2,1)S(1)} %copy-done.39, f32[2048,1024]{1,0:T(8,128)} %copy-done.11), kind=kOutput, calls=%fused_computation.56 | convolution fusion | flops 1093664768 | bytes 12058624 | tf_op jit(solution)/shard_map/dot_general | solution.py:135
  168.4 1.8 fusion.68
  170.2 2.3 copy.95
  172.5 1.7 fusion.37
  174.2 1.5 concatenate.28
  175.7 2.9 copy.93
  178.6 1.7 fusion.35
  180.3 1.5 concatenate.29
  181.7 3.3 copy.94
  185.1 3.6 fusion.26
  190.3 2.5 copy.89
  192.9 11.5 %scatter_custom_fusion.2 = bf16[2048,512]{1,0:T(8,128)(2,1)} fusion(s32[2048]{0:T(1024)S(1)} %bitcast.160, bf16[2048,512]{1,0:T(8,128)(2,1)} %copy.89, bf16[]{:T(256)} %constant.59.clone.1), kind=kCustom, calls=%fused_computation.107 | custom fusion | bytes 2097664 | tf_op jit(solution)/shard_map/scatter | solution.py:251
  204.3 4.4 all-to-all-start.1
  208.8 2.1 convolution_bitcast_fusion.2
  211.9 1.8 copy.99
  216.3 1.5 constant_dynamic-update-slice_fusion.8
  217.8 2.6 constant_dynamic-update-slice_fusion.7
  220.4 2.4 constant_dynamic-update-slice_fusion.6
  223.0 16.4 %all-to-all-done.1 = bf16[128,16,512]{2,1,0:T(8,128)(2,1)S(1)} async-done(((bf16[128,16,512]{2,1,0:T(8,128)(2,1)}), bf16[128,16,512]{2,1,0:T(8,128)(2,1)S(1)}, u32[]{:S(2)}, u32[]{:S(2)}) %all-to-all-start.1) | async-done | bytes 2097184 | tf_op jit(solution)/shard_map/all_to_all | solution.py:252
  239.3 5.1 gather_fusion.4
  244.4 1.5 broadcast_select_fusion.1
  249.0 1.9 fusion.50
  250.9 34.5 %all-reduce.8.cloned.1.call-done = f32[549376]{0:T(1024)} async-done(((f32[549376]{0:T(1024)}), f32[549376]{0:T(1024)}) %all-reduce.8.cloned.1.call-update) | async-done | bytes 2197520 | tf_op jit(solution)/shard_map/psum | solution.py:259
  285.6 4.0 fusion.74
  289.6 2.0 collective-permute-start.4
  291.6 1.5 collective-permute-start.5
  293.0 4.0 collective-permute-start.6
  297.0 1.9 collective-permute-start.7
  300.0 2.2 convert_add_fusion.1
  303.0 3.1 scatter_custom_fusion.3
  306.1 3.1 scatter_custom_fusion.4
  309.1 3.1 scatter_custom_fusion.5
  312.2 3.1 scatter_custom_fusion.6
  315.3 80.3 %all-reduce.10.cloned.1.call-done = f32[549376]{0:T(1024)} async-done(((f32[549376]{0:T(1024)}), f32[549376]{0:T(1024)}) %all-reduce.10.cloned.1.call-update) | async-done | bytes 2197520 | tf_op jit(solution)/shard_map/psum | solution.py:259
  395.6 2.7 slice_multiply_fusion
  399.2 2.4 mul.316
  406.0 140.3 %all-reduce.12.cloned.1.call-done = f32[256,256]{1,0:T(8,128)} async-done(((f32[256,256]{1,0:T(8,128)}), f32[256,256]{1,0:T(8,128)}) %all-reduce.12.cloned.1.call-update) | async-done | bytes 262160 | tf_op jit(solution)/shard_map/psum | solution.py:272
  546.3 1.7 broadcast_multiply_fusion
  (165 shorter events, 34.5 us)
Async XLA Ops:
  7.2 128.4 %copy-start = (bf16[256,1024]{1,0:T(8,128)(2,1)S(1)}, bf16[256,1024]{1,0:T(8,128)(2,1)}, u32[]{:S(2)}) copy-start(bf16[256,1024]{1,0:T(8,128)(2,1)} %param.23) | copy-start | bytes 1572868
  7.2 7.3 %copy-start.2 = (s32[1,1024]{1,0:T(1,128)S(1)}, s32[1,1024]{1,0:T(1,128)}, u32[]{:S(2)}) copy-start(s32[1,1024]{1,0:T(1,128)} %param.15) | copy-start | bytes 12292
  14.5 4.6 copy-start.18
  19.1 13.8 %copy-start.33 = (s32[1,16,1024]{2,1,0:T(8,128)S(1)}, s32[1,16,1024]{2,1,0:T(8,128)}, u32[]{:S(2)}) copy-start(s32[1,16,1024]{2,1,0:T(8,128)} %param.18) | copy-start | bytes 196612
  20.4 34.9 %collective-permute-start = (bf16[64,256]{1,0:T(8,128)(2,1)S(1)}, bf16[64,256]{1,0:T(8,128)(2,1)S(1)}, u32[]{:S(2)}, u32[]{:S(2)}) collective-permute-start(bf16[64,256]{1,0:T(8,128)(2,1)S(1)} %get-tuple-element.62), channel_id=1, source_target_pairs={{32,0},{64,32},{96,64},{33,1},{65,33},{97,65},{34,2},{66,34},{98,6... | collective-permute-start | bytes 98312 | tf_op jit(solution)/shard_map/ppermute | solution.py:16
  21.7 33.6 %collective-permute-start.1 = (bf16[64,256]{1,0:T(8,128)(2,1)S(1)}, bf16[64,256]{1,0:T(8,128)(2,1)S(1)}, u32[]{:S(2)}, u32[]{:S(2)}) collective-permute-start(bf16[64,256]{1,0:T(8,128)(2,1)S(1)} %get-tuple-element.61), channel_id=1, source_target_pairs={{0,32},{32,64},{64,96},{1,33},{33,65},{65,97},{2,34},{34,66},{66,9... | collective-permute-start | bytes 98312 | tf_op jit(solution)/shard_map/ppermute | solution.py:16
  26.7 28.6 %collective-permute-start.2 = (bf16[64,256]{1,0:T(8,128)(2,1)S(1)}, bf16[64,256]{1,0:T(8,128)(2,1)S(1)}, u32[]{:S(2)}, u32[]{:S(2)}) collective-permute-start(bf16[64,256]{1,0:T(8,128)(2,1)S(1)} %get-tuple-element.60), channel_id=1, source_target_pairs={{1,0},{2,1},{3,2},{4,3},{5,4},{6,5},{7,6},{8,7},{9,8},{10,9},{11,1... | collective-permute-start | bytes 98312 | tf_op jit(solution)/shard_map/ppermute | solution.py:16
  29.6 25.7 %collective-permute-start.3 = (bf16[64,256]{1,0:T(8,128)(2,1)S(1)}, bf16[64,256]{1,0:T(8,128)(2,1)S(1)}, u32[]{:S(2)}, u32[]{:S(2)}) collective-permute-start(bf16[64,256]{1,0:T(8,128)(2,1)S(1)} %get-tuple-element.59), channel_id=1, source_target_pairs={{0,1},{1,2},{2,3},{3,4},{4,5},{5,6},{6,7},{7,8},{8,9},{9,10},{10,1... | collective-permute-start | bytes 98312 | tf_op jit(solution)/shard_map/ppermute | solution.py:16
  55.2 1.6 copy-start.3
  55.3 1.4 copy-start.31
  56.8 1.5 copy-start.27
  56.8 1.5 copy-start.29
  65.1 11.2 %copy-start.30 = (bf16[3,8,32,32]{3,2,1,0:T(8,128)(2,1)S(1)}, bf16[3,8,32,32]{3,2,1,0:T(8,128)(2,1)}, u32[]{:S(2)}) copy-start(bf16[3,8,32,32]{3,2,1,0:T(8,128)(2,1)} %param.21) | copy-start | bytes 147460
  65.1 41.7 %all-to-all-start = ((bf16[128,16,512]{2,1,0:T(8,128)(2,1)}), bf16[128,16,512]{2,1,0:T(8,128)(2,1)S(1)}, u32[]{:S(2)}, u32[]{:S(2)}) async-start(bf16[128,16,512]{2,1,0:T(8,128)(2,1)} %bitcast.148), calls=%async_computation | async-start | bytes 4194304 | tf_op jit(solution)/shard_map/all_to_all | solution.py:235
  77.6 5.7 %copy-start.34 = (s32[1,2048]{1,0:T(1,128)S(1)}, s32[1,2048]{1,0:T(1,128)}, u32[]{:S(2)}) copy-start(s32[1,2048]{1,0:T(1,128)} %param.16) | copy-start | bytes 24580
  119.9 2.1 copy-start.37
  131.6 1.2 copy-start.12
  131.9 1.2 copy-start.26
  132.8 1.0 copy-start.13
  133.0 1.3 copy-start.9
  134.9 0.7 copy-start.36
  135.6 10.1 %copy-start.5 = (f32[2048,256]{0,1:T(8,128)}, f32[2048,256]{0,1:T(8,128)S(1)}, u32[]{:S(2)}) copy-start(f32[2048,256]{0,1:T(8,128)S(1)} %get-tuple-element.88) | copy-start | bytes 6291460
  135.6 1.4 copy-start.38
  137.1 6.3 %copy-start.11 = (f32[2048,1024]{1,0:T(8,128)}, f32[2048,1024]{1,0:T(8,128)S(1)}, u32[]{:S(2)}) copy-start(f32[2048,1024]{1,0:T(8,128)S(1)} %fusion.67) | copy-start | bytes 25165828
  153.6 6.4 %copy-start.6 = (f32[2048,256]{0,1:T(8,128)S(1)}, f32[2048,256]{0,1:T(8,128)}, u32[]{:S(2)}) copy-start(f32[2048,256]{0,1:T(8,128)} %copy-done.5) | copy-start | bytes 6291460
  153.6 6.4 %copy-start.39 = (bf16[1024,256]{1,0:T(8,128)(2,1)S(1)}, bf16[1024,256]{1,0:T(8,128)(2,1)}, u32[]{:S(2)}) copy-start(bf16[1024,256]{1,0:T(8,128)(2,1)} %param.24) | copy-start | bytes 1572868
  160.0 6.9 %copy-start.24 = (f32[32,8,8,128]{3,2,1,0:T(8,128)S(1)}, f32[32,8,8,128]{3,2,1,0:T(8,128)}, u32[]{:S(2)}) copy-start(f32[32,8,8,128]{3,2,1,0:T(8,128)} %convolution_bitcast_fusion.1) | copy-start | bytes 3145732
  166.9 1.5 copy-start.21
  185.0 3.7 copy-start.7
  185.0 3.7 copy-start.22
  188.7 1.4 copy-start.25
  204.3 35.0 %all-to-all-start.1 = ((bf16[128,16,512]{2,1,0:T(8,128)(2,1)}), bf16[128,16,512]{2,1,0:T(8,128)(2,1)S(1)}, u32[]{:S(2)}, u32[]{:S(2)}) async-start(bf16[128,16,512]{2,1,0:T(8,128)(2,1)} %bitcast.147), calls=%async_computation.1 | async-start | bytes 4194304 | tf_op jit(solution)/shard_map/all_to_all | solution.py:252
  208.7 76.8 %all-reduce.8.cloned.1.call-start = ((), (), s32[]{:S(2)}) async-start(), calls=%async_computation.2 | async-start | bytes 4399104 | tf_op jit(solution)/shard_map/psum | solution.py:259
  208.7 2.1 copy-start.8
  208.7 2.2 copy-start.19
  208.8 2.6 copy-start.10
  220.4 2.5 copy-start.35
  222.9 172.7 %all-reduce.10.cloned.1.call-start = ((), (), s32[]{:S(2)}) async-start(), calls=%async_computation.3 | async-start | bytes 4399104 | tf_op jit(solution)/shard_map/psum | solution.py:259
  244.4 2.5 copy-start.23
  244.4 3.2 copy-start.32
  246.0 1.0 copy-start.16
  246.0 3.0 copy-start.4
  248.0 1.0 copy-start.14
  285.5 260.8 %all-reduce.12.cloned.1.call-start = ((), (), s32[]{:S(2)}) async-start(), calls=%async_computation.4 | async-start | bytes 524288 | tf_op jit(solution)/shard_map/psum | solution.py:272
  285.5 13.4 %copy-start.28 = (bf16[1024,256]{1,0:T(8,128)(2,1)S(1)}, bf16[1024,256]{1,0:T(8,128)(2,1)}, u32[]{:S(2)}) copy-start(bf16[1024,256]{1,0:T(8,128)(2,1)} %copy-done.27) | copy-start | bytes 1572868
  289.5 10.4 %copy-start.15 = (f32[1280,256]{1,0:T(8,128)S(1)}, f32[1280,256]{1,0:T(8,128)}, u32[]{:S(2)}) copy-start(f32[1280,256]{1,0:T(8,128)} %get-tuple-element.92) | copy-start | bytes 3932164
  289.5 12.6 %copy-start.17 = (bf16[1024,512]{1,0:T(8,128)(2,1)S(1)}, bf16[1024,512]{1,0:T(8,128)(2,1)}, u32[]{:S(2)}) copy-start(bf16[1024,512]{1,0:T(8,128)(2,1)} %copy-done.16) | copy-start | bytes 3145732
  289.6 13.4 %collective-permute-start.4 = (bf16[64,256]{1,0:T(8,128)(2,1)S(1)}, bf16[64,256]{1,0:T(8,128)(2,1)S(1)}, u32[]{:S(2)}, u32[]{:S(2)}) collective-permute-start(bf16[64,256]{1,0:T(8,128)(2,1)S(1)} %get-tuple-element.58), channel_id=1, source_target_pairs={{0,32},{32,64},{64,96},{1,33},{33,65},{65,97},{2,34},{34,66},{66,9... | collective-permute-start | bytes 98312 | tf_op jit(solution)/shard_map/ppermute | solution.py:16
  291.6 14.5 %collective-permute-start.5 = (bf16[64,256]{1,0:T(8,128)(2,1)S(1)}, bf16[64,256]{1,0:T(8,128)(2,1)S(1)}, u32[]{:S(2)}, u32[]{:S(2)}) collective-permute-start(bf16[64,256]{1,0:T(8,128)(2,1)S(1)} %get-tuple-element.57), channel_id=1, source_target_pairs={{32,0},{64,32},{96,64},{33,1},{65,33},{97,65},{34,2},{66,34},{98,6... | collective-permute-start | bytes 98312 | tf_op jit(solution)/shard_map/ppermute | solution.py:16
  293.0 16.1 %collective-permute-start.6 = (bf16[64,256]{1,0:T(8,128)(2,1)S(1)}, bf16[64,256]{1,0:T(8,128)(2,1)S(1)}, u32[]{:S(2)}, u32[]{:S(2)}) collective-permute-start(bf16[64,256]{1,0:T(8,128)(2,1)S(1)} %get-tuple-element.56), channel_id=1, source_target_pairs={{0,1},{1,2},{2,3},{3,4},{4,5},{5,6},{6,7},{7,8},{8,9},{9,10},{10,1... | collective-permute-start | bytes 98312 | tf_op jit(solution)/shard_map/ppermute | solution.py:16
  297.0 15.2 %collective-permute-start.7 = (bf16[64,256]{1,0:T(8,128)(2,1)S(1)}, bf16[64,256]{1,0:T(8,128)(2,1)S(1)}, u32[]{:S(2)}, u32[]{:S(2)}) collective-permute-start(bf16[64,256]{1,0:T(8,128)(2,1)S(1)} %get-tuple-element.55), channel_id=1, source_target_pairs={{1,0},{2,1},{3,2},{4,3},{5,4},{6,5},{7,6},{8,7},{9,8},{10,9},{11,1... | collective-permute-start | bytes 98312 | tf_op jit(solution)/shard_map/ppermute | solution.py:16
  399.2 3.7 copy-start.20
  401.7 146.3 %copy-start.1 = (bf16[256,1024]{1,0:T(8,128)(2,1)S(1)}, bf16[256,1024]{1,0:T(8,128)(2,1)}, u32[]{:S(2)}) copy-start(bf16[256,1024]{1,0:T(8,128)(2,1)} %param.23) | copy-start | bytes 1572868
Sparse Core Ops, SparseCore 0:
  223.0 62.4 all-reduce.7
  288.8 106.7 all-reduce.9
  404.8 141.4 all-reduce.11
